TPU v7x, 32 devices: a whole 2x2x4 slice. The times are simulated.
32 devices in a mesh: row: 16 (over z, x, core), col: 2 (over y).
Axes of the slice: x: 2, y: 2, z: 4, core: 2. Of those that a mesh axis runs over, the one named last changes fastest.
Arguments:
- counts: float32 [8192, 8192], P('row', 'col'), may hold values from 0 to 12, as said below
- loadings: float32 [8192, 64], P(('col', 'row')), may hold values from 0.02 to 0.4
Outputs:
- row_grad: float32 [8192, 64], P(('row', 'col'))
- col_grad: float32 [8192, 64], P(('col', 'row'))
Inputs may be any that keep to these rules, and one draw needn't show every extreme that they name: `counts`: whole numbers, more of them near the diagonal.
All inputs are finite; a program needn't handle non-finite values.
Results may differ from a plain program's by a relative error of at most 0.0003.
Values sent between devices are 32-bit elements; how exact they have to be, the bound alone decides.
A program may use at most 64 MiB of HBM per device.

v0:
```python
import jax
import jax.numpy as jnp
from jax import lax
from jax.sharding import PartitionSpec as P


def broadcast(block, axis, source):
    block = jnp.where(lax.axis_index(axis) == source, block, jnp.zeros_like(block))
    return lax.psum(block, axis)


def shards(counts, loadings):
    rows = counts.shape[0]
    cols = counts.shape[1]
    nrow = lax.axis_size("row")
    ncol = lax.axis_size("col")
    nbins = rows * nrow
    scale = 1.0 / nbins**0.5
    row_index = lax.axis_index("row")
    col_index = lax.axis_index("col")
    colblock = lax.all_gather(loadings, "row", axis=0, tiled=True)
    group = nrow // ncol
    offset = row_index % group * rows
    portion = lax.dynamic_slice_in_dim(colblock, offset, rows, 0)
    rowblock = broadcast(portion, "col", row_index // group)
    rate = jnp.dot(rowblock, colblock.T, precision=lax.Precision.HIGHEST)
    positions = row_index * rows + jnp.arange(rows)
    targets = col_index * cols + jnp.arange(cols)
    keep = jnp.abs(positions[:, None] - targets[None, :]) >= 2
    ratio = jnp.where(keep, 1.0 - counts / rate, jnp.float32(0.0))
    slab = ratio
    row_grad = lax.psum_scatter(
        jnp.dot(slab, colblock, precision=lax.Precision.HIGHEST) * scale,
        "col",
        scatter_dimension=0,
        tiled=True,
    )
    slab = ratio
    col_grad = lax.psum_scatter(
        jnp.einsum("ij,ik->jk", slab, rowblock, precision=lax.Precision.HIGHEST) * scale,
        "row",
        scatter_dimension=0,
        tiled=True,
    )
    return (row_grad, col_grad)


def solution(mesh):
    placed = (P("row", "col"), P(("col", "row"), None))
    return jax.shard_map(
        shards,
        mesh=mesh,
        in_specs=placed,
        out_specs=(P(("row", "col"), None), P(("col", "row"), None)),
        check_vma=False,
    )
```

profile of v0, /device:TPU:0, one launch (start us, length us, event | category | flops | bytes accessed | tf_op | source)
XLA Modules:
  0.0 175.3 jit_solution(6677871117199778213)
XLA Ops:
  7.2 0.0 all-gather.2.cloned.1.call-start
  7.2 0.7 all-gather.2.cloned.1.call-update
  7.9 0.0 all-reduce.2.cloned.1.call-start
  8.0 41.6 %all-gather.2.cloned.1.call-done = f32[4096,64]{0,1:T(8,128)} async-done(((f32[256,64]{0,1:T(8,128)}), f32[4096,64]{0,1:T(8,128)}) %all-gather.2.cloned.1.call-update) | async-done | bytes 1048592 | tf_op jit(solution)/shard_map/all_gather | solution.py:21
  49.5 1.6 dynamic-slice_select_fusion
  51.1 0.0 all-reduce.2.cloned.1.call-update
  51.1 0.0 reduce-scatter.3.cloned.1.call-start
  51.2 0.0 copy-start.1
  51.2 21.7 %all-reduce.2.cloned.1.call-done = f32[512,64]{0,1:T(8,128)} async-done(((f32[512,64]{0,1:T(8,128)}), f32[512,64]{0,1:T(8,128)}) %all-reduce.2.cloned.1.call-update) | async-done | bytes 131088 | tf_op jit(solution)/shard_map/psum | solution.py:9
  73.0 11.5 %subtract_select_fusion = f32[512,4096]{1,0:T(8,128)S(1)} fusion(f32[512,4096]{1,0:T(8,128)} %param.2, f32[512,64]{0,1:T(8,128)} %all-reduce.2.cloned.1.call-done, f32[4096,64]{0,1:T(8,128)} %all-gather.2.cloned.1.call-done, s32[4096]{0:T(1024)S(1)} %iota_add_fusion, s32[512]{0:T(512)S(1)} %iota_add_fusion.1), kind=kOutput, calls=%fused_computation | convolution fusion | flops 1623195648 | bytes 17975296 | tf_op jit(solution)/shard_map/dot_general | solution.py:26
  84.5 0.0 copy-start
  84.5 3.2 %copy-done = f32[512,4096]{1,0:T(8,128)} copy-done((f32[512,4096]{1,0:T(8,128)}, f32[512,4096]{1,0:T(8,128)S(1)}, u32[]{:S(2)}) %copy-start) | copy-done | bytes 8388632
  87.7 0.0 copy-done.1
  87.7 0.0 copy-start.2
  87.7 8.9 %convolution_multiply_fusion.1 = f32[512,64]{0,1:T(8,128)} fusion(f32[512,4096]{1,0:T(8,128)S(1)} %subtract_select_fusion, f32[4096,64]{0,1:T(8,128)S(1)} %copy-done.1), kind=kOutput, calls=%fused_computation.3 | convolution fusion | flops 1610645504 | bytes 9568256 | tf_op jit(solution)/shard_map/dot_general | solution.py:33
  96.6 0.0 reduce-scatter.3.cloned.1.call-update
  96.6 0.2 reduce-scatter.5.cloned.1.call-start
  96.8 0.0 copy-done.2
  96.8 9.0 %convolution_multiply_fusion = f32[4096,64]{0,1:T(8,128)} fusion(f32[512,4096]{1,0:T(8,128)} %copy-done, f32[512,64]{0,1:T(8,128)S(1)} %copy-done.2), kind=kOutput, calls=%fused_computation.2 | convolution fusion | flops 1610874880 | bytes 9568256 | tf_op jit(solution)/shard_map/ij,ik->jk/dot_general | solution.py:40
  105.9 0.0 reduce-scatter.5.cloned.1.call-update
  105.9 1.2 reduce-scatter.3.cloned.1.call-done
  107.1 61.6 %reduce-scatter.5.cloned.1.call-done = f32[256,64]{0,1:T(8,128)} async-done(((f32[4096,64]{0,1:T(8,128)}), f32[256,64]{0,1:T(8,128)}) %reduce-scatter.5.cloned.1.call-update) | async-done | bytes 65552 | tf_op jit(solution)/shard_map/reduce_scatter | solution.py:39
  (2 shorter events, 0.0 us)
Async XLA Ops:
  7.2 42.4 %all-gather.2.cloned.1.call-start = ((), (), s32[]{:S(2)}) async-start(), calls=%async_computation.2 | async-start | bytes 1114112 | tf_op jit(solution)/shard_map/all_gather | solution.py:21
  7.9 65.1 %all-reduce.2.cloned.1.call-start = ((), (), s32[]{:S(2)}) async-start(), calls=%async_computation.3 | async-start | bytes 262144 | tf_op jit(solution)/shard_map/psum | solution.py:9
  51.1 56.0 %reduce-scatter.3.cloned.1.call-start = ((), (), s32[]{:S(2)}) async-start(), calls=%async_computation.4 | async-start | bytes 196608 | tf_op jit(solution)/shard_map/reduce_scatter | solution.py:32
  51.2 36.5 %copy-start.1 = (f32[4096,64]{0,1:T(8,128)S(1)}, f32[4096,64]{0,1:T(8,128)}, u32[]{:S(2)}) copy-start(f32[4096,64]{0,1:T(8,128)} %all-gather.2.cloned.1.call-done) | copy-start | bytes 3145732
  84.5 3.2 %copy-start = (f32[512,4096]{1,0:T(8,128)}, f32[512,4096]{1,0:T(8,128)S(1)}, u32[]{:S(2)}) copy-start(f32[512,4096]{1,0:T(8,128)S(1)} %subtract_select_fusion) | copy-start | bytes 25165828
  87.7 9.1 %copy-start.2 = (f32[512,64]{0,1:T(8,128)S(1)}, f32[512,64]{0,1:T(8,128)}, u32[]{:S(2)}) copy-start(f32[512,64]{0,1:T(8,128)} %all-reduce.2.cloned.1.call-done) | copy-start | bytes 393220
  96.6 72.2 %reduce-scatter.5.cloned.1.call-start = ((), (), s32[]{:S(2)}) async-start(), calls=%async_computation.5 | async-start | bytes 1114112 | tf_op jit(solution)/shard_map/reduce_scatter | solution.py:39
Sparse Core Ops, SparseCore 0:
  10.1 39.3 all-gather.1
  51.8 21.1 all-reduce.1
  96.7 10.3 reduce-scatter.2
  111.2 57.5 reduce-scatter.4
where the time goes:
time: 175 us
  waiting for transfers between devices  127 us (73%)
  matrix products  29.4 us (17%)
  between operations  13.8 us (8%)
  local copies, waits for them, and re-layouts  3.22 us (2%)
    reduce_scatter x1, waiting for transfers between devices, shards(): lax.psum_scatter(jnp.einsum('ij,ik->jk', slab, rowblock, precision=lax.Pr...  61.6 us
    all_gather x1, waiting for transfers between devices, shards(): colblock = lax.all_gather(loadings, 'row', axis=0, tiled=True)  41.6 us
    psum x1, waiting for transfers between devices, broadcast(): return lax.psum(block, axis)  21.7 us
    dot_general x1, matrix products, shards(): rate = jnp.dot(rowblock, colblock.T, precision=lax.Precision.HIGHEST)  11.5 us
    dot_general x1, matrix products, shards(): jnp.einsum('ij,ik->jk', slab, rowblock, precision=lax.Precision.HIGHEST)  9.02 us
    dot_general x1, matrix products, shards(): jnp.dot(slab, colblock, precision=lax.Precision.HIGHEST) * scale  8.88 us
  transfers between devices with their start and end apart: 4, of which 4 were waited for; matrix products, arithmetic and copies ran while one was open for 5% of the time, Pallas kernels for 0%

commit v1 on v0

--- a/solution.py
+++ b/solution.py
@@ -4,9 +4,15 @@
 from jax.sharding import PartitionSpec as P
 
 
+def summed_here(array, axis):
+    parts = lax.all_gather(array, axis, axis=0, tiled=False)
+    summed = parts.sum(axis=0)
+    return summed
+
+
 def broadcast(block, axis, source):
     block = jnp.where(lax.axis_index(axis) == source, block, jnp.zeros_like(block))
-    return lax.psum(block, axis)
+    return summed_here(block, axis)
 
 
 def shards(counts, loadings):

time: 175 us -> 160 us (0.914)
  waiting for transfers between devices: 127 us -> 105 us
  blocking collectives: 0 us -> 6.31 us
    psum x1 -> x0, waiting for transfers between devices: 21.7 us -> none  [broadcast(): return lax.psum(block, axis)]
    all_gather x0 -> x1, blocking collectives: none -> 6.31 us  [summed_here(): parts = lax.all_gather(array, axis, axis=0, tiled=False)]
  transfers between devices with their start and end apart: 4 -> 3, of which waited for: 4 -> 3; matrix products, arithmetic and copies ran while one was open for 5% -> 6% of each run, Pallas kernels for 0% -> 0%
where the time goes in v1:
time: 160 us
  waiting for transfers between devices  105 us (66%)
  matrix products  29.5 us (18%)
  between operations  13.8 us (9%)
  blocking collectives  6.31 us (4%)
  local copies, waits for them, and re-layouts  3.44 us (2%)
    reduce_scatter x1, waiting for transfers between devices, shards(): lax.psum_scatter(jnp.einsum('ij,ik->jk', slab, rowblock, precision=lax.Pr...  61.8 us
    all_gather x1, waiting for transfers between devices, shards(): colblock = lax.all_gather(loadings, 'row', axis=0, tiled=True)  41.5 us
    dot_general x1, matrix products, shards(): rate = jnp.dot(rowblock, colblock.T, precision=lax.Precision.HIGHEST)  11.6 us
    dot_general x1, matrix products, shards(): jnp.einsum('ij,ik->jk', slab, rowblock, precision=lax.Precision.HIGHEST)  9 us
    dot_general x1, matrix products, shards(): jnp.dot(slab, colblock, precision=lax.Precision.HIGHEST) * scale  8.92 us
    all_gather x1, blocking collectives, summed_here(): parts = lax.all_gather(array, axis, axis=0, tiled=False)  6.31 us
    unnamed x4, local copies, waits for them, and re-layouts  3.22 us
  transfers between devices with their start and end apart: 3, of which 3 were waited for; matrix products, arithmetic and copies ran while one was open for 6% of the time, Pallas kernels for 0%

profile of v1, /device:TPU:0, one launch (start us, length us, event | category | flops | bytes accessed | tf_op | source)
XLA Modules:
  0.0 159.6 jit_solution(16490301196389030746)
XLA Ops:
  7.2 0.0 all-gather.3.cloned.1.call-start
  7.2 0.7 all-gather.3.cloned.1.call-update
  7.9 0.0 reduce-scatter.3.cloned.1.call-start
  8.0 41.5 %all-gather.3.cloned.1.call-done = f32[4096,64]{0,1:T(8,128)} async-done(((f32[256,64]{0,1:T(8,128)}), f32[4096,64]{0,1:T(8,128)}) %all-gather.3.cloned.1.call-update) | async-done | bytes 1048592 | tf_op jit(solution)/shard_map/all_gather | solution.py:27
  49.5 0.9 dynamic-slice_select_fusion
  50.4 6.3 %all-gather = f32[1024,64]{0,1:T(8,128)S(1)} all-gather(f32[512,64]{0,1:T(8,128)S(1)} %dynamic-slice_select_fusion), channel_id=2, replica_groups=mesh['row'=16,'col'=2] {'col'}, dimensions={0}, use_global_device_ids=true | all-gather | bytes 393216 | tf_op jit(solution)/shard_map/all_gather | solution.py:8
  56.8 0.2 reshape.12
  57.0 0.3 reduce_sum.9
  57.3 0.0 copy-start.1
  57.3 11.6 %subtract_select_fusion = f32[512,4096]{1,0:T(8,128)S(1)} fusion(f32[512,4096]{1,0:T(8,128)} %param.2, f32[512,64]{0,1:T(8,128)S(1)} %reduce_sum.9, f32[4096,64]{0,1:T(8,128)} %all-gather.3.cloned.1.call-done, s32[4096]{0:T(1024)S(1)} %iota_add_fusion, s32[512]{0:T(512)S(1)} %iota_add_fusion.1), kind=kOutput, calls=%fused_computation | convolution fusion | flops 1623195648 | bytes 17975296 | tf_op jit(solution)/shard_map/dot_general | solution.py:32
  68.9 0.0 copy-start
  68.9 3.2 %copy-done = f32[512,4096]{1,0:T(8,128)} copy-done((f32[512,4096]{1,0:T(8,128)}, f32[512,4096]{1,0:T(8,128)S(1)}, u32[]{:S(2)}) %copy-start) | copy-done | bytes 8388632
  72.1 0.0 copy-done.1
  72.1 8.9 %convolution_multiply_fusion.1 = f32[512,64]{0,1:T(8,128)} fusion(f32[512,4096]{1,0:T(8,128)S(1)} %subtract_select_fusion, f32[4096,64]{0,1:T(8,128)S(1)} %copy-done.1), kind=kOutput, calls=%fused_computation.3 | convolution fusion | flops 1610645504 | bytes 9568256 | tf_op jit(solution)/shard_map/dot_general | solution.py:39
  81.0 0.0 reduce-scatter.3.cloned.1.call-update
  81.1 0.2 reduce-scatter.5.cloned.1.call-start
  81.3 9.0 %convolution_multiply_fusion = f32[4096,64]{0,1:T(8,128)} fusion(f32[512,4096]{1,0:T(8,128)} %copy-done, f32[512,64]{0,1:T(8,128)S(1)} %reduce_sum.9), kind=kOutput, calls=%fused_computation.2 | convolution fusion | flops 1610874880 | bytes 9568256 | tf_op jit(solution)/shard_map/ij,ik->jk/dot_general | solution.py:46
  90.3 0.0 reduce-scatter.5.cloned.1.call-update
  90.3 0.9 reduce-scatter.3.cloned.1.call-done
  91.2 61.8 %reduce-scatter.5.cloned.1.call-done = f32[256,64]{0,1:T(8,128)} async-done(((f32[4096,64]{0,1:T(8,128)}), f32[256,64]{0,1:T(8,128)}) %reduce-scatter.5.cloned.1.call-update) | async-done | bytes 65552 | tf_op jit(solution)/shard_map/reduce_scatter | solution.py:45
  (2 shorter events, 0.0 us)
Async XLA Ops:
  7.2 42.4 %all-gather.3.cloned.1.call-start = ((), (), s32[]{:S(2)}) async-start(), calls=%async_computation.2 | async-start | bytes 1114112 | tf_op jit(solution)/shard_map/all_gather | solution.py:27
  7.9 83.3 %reduce-scatter.3.cloned.1.call-start = ((), (), s32[]{:S(2)}) async-start(), calls=%async_computation.3 | async-start | bytes 196608 | tf_op jit(solution)/shard_map/reduce_scatter | solution.py:38
  57.3 14.8 %copy-start.1 = (f32[4096,64]{0,1:T(8,128)S(1)}, f32[4096,64]{0,1:T(8,128)}, u32[]{:S(2)}) copy-start(f32[4096,64]{0,1:T(8,128)} %all-gather.3.cloned.1.call-done) | copy-start | bytes 3145732
  68.9 3.2 %copy-start = (f32[512,4096]{1,0:T(8,128)}, f32[512,4096]{1,0:T(8,128)S(1)}, u32[]{:S(2)}) copy-start(f32[512,4096]{1,0:T(8,128)S(1)} %subtract_select_fusion) | copy-start | bytes 25165828
  81.1 72.0 %reduce-scatter.5.cloned.1.call-start = ((), (), s32[]{:S(2)}) async-start(), calls=%async_computation.4 | async-start | bytes 1114112 | tf_op jit(solution)/shard_map/reduce_scatter | solution.py:45
Sparse Core Ops, SparseCore 0:
  10.1 39.3 all-gather.2
  81.2 9.9 reduce-scatter.2
  95.4 57.6 reduce-scatter.4
